TPU v7x, 32 devices: a whole 2x2x4 slice. The times are simulated.
32 devices in a mesh: dp: 8 (over z, x), seq: 4 (over y, core).
Axes of the slice: x: 2, y: 2, z: 4, core: 2. Of those that a mesh axis runs over, the one named last changes fastest.
Arguments:
- hidden_states: bfloat16 [8, 2, 1024, 1024], P('dp', None, 'seq'), may hold values from -8.5 to 8.5
- lengths: int32 [8, 2], P('dp'), may hold values from 256 to 1024, as said below
- w_query: bfloat16 [1024, 1024], replicated, may hold values from -0.1875 to 0.1875
- w_key: bfloat16 [1024, 1024], replicated, may hold values from -0.1875 to 0.1875
- w_value: bfloat16 [1024, 1024], replicated, may hold values from -0.1875 to 0.1875
- w_out: bfloat16 [1024, 1024], replicated, may hold values from -0.1875 to 0.1875
- running_cov: float32 [1024, 1024], P('seq'), as said below
Outputs:
- whitened: float32 [8, 2, 1024], P('dp')
- cov_new: float32 [1024, 1024], P('seq')
- loss: float32 [], replicated
Inputs may be any that keep to these rules, and one draw needn't show every extreme that they name: `lengths`: at least a quarter of a module is valid; some module has all 1024 tokens valid. `running_cov`: Symmetric, with a diagonal larger than the sum of the magnitudes of its row's other entries.
All inputs are finite; a program needn't handle non-finite values.
Results may differ from a plain program's by a relative error of at most 0.0037.
The roundings to bfloat16 on the way count: a program that leaves them out, or rounds other values in their place, can miss the bound.
Values sent between devices are 32-bit elements; how exact they have to be, the bound alone decides.
No kernel may reach another device: no remote copies, remote signals or barrier semaphores. Data moves between devices by JAX's collectives and lax.ppermute only.
A program may use at most 128 MiB of HBM per device.

v0:
```python
import jax
import jax.numpy as jnp
from jax import lax
from jax.sharding import PartitionSpec as P

HEADS = 16
HEAD_DIM = 64


def passed_along(array, axis, by):
    size = lax.axis_size(axis)
    pairs = [(i, i + by) for i in range(size) if 0 <= i + by < size]
    return lax.ppermute(array, axis, pairs)


def feature(u):
    return jnp.where(u > 0.0, u + 1.0, jnp.exp(jnp.minimum(u, 0.0)))


def whiten_rows(full_cov, sum_embed, second, total, rows_in):
    mean = sum_embed / total
    batch_cov = (second - total * mean[:, None] * mean[None, :]) / (total - 1)
    cov_full = 0.5 * full_cov + 0.5 * batch_cov
    chol = jnp.linalg.cholesky(cov_full)
    result = lax.linalg.triangular_solve(chol, (rows_in - mean).T, left_side=True, lower=True).T
    return (cov_full, result)


def pair_terms(whitened_rows):
    normed = whitened_rows / jnp.sqrt(
        jnp.sum(whitened_rows * whitened_rows, axis=1, keepdims=True) + 1e-06
    )
    normed = normed.reshape(-1, 2, normed.shape[1])
    gap = normed[:, 0] - normed[:, 1]
    return jnp.sum(gap * gap)


def body(hidden_states, lengths, w_query, w_key, w_value, w_out, running_cov):
    pairs, two, span, width = hidden_states.shape
    count = pairs * two
    heads = HEADS
    head_dim = HEAD_DIM
    rows = hidden_states.reshape(count * span, width)

    def project(weight):
        return jnp.dot(rows, weight, preferred_element_type=jnp.float32)

    f_query = feature(project(w_query)).astype(jnp.bfloat16).reshape(count, span, heads, head_dim)
    f_key = feature(project(w_key)).astype(jnp.bfloat16).reshape(count, span, heads, head_dim)
    values = project(w_value).astype(jnp.bfloat16).reshape(count, span, heads, head_dim)
    local_state = jnp.einsum("slhe,slhf->shef", f_key, values, preferred_element_type=jnp.float32)
    local_norm = jnp.sum(f_key.astype(jnp.float32), axis=1)
    empty_state = jnp.zeros_like(local_state)
    empty_norm = jnp.zeros_like(local_norm)

    def relay(step, carried):
        return passed_along((carried[0] + local_state, carried[1] + local_norm), "seq", 1)

    prior_state, prior_norm = lax.fori_loop(
        0, lax.axis_size("seq") - 1, relay, (empty_state, empty_norm)
    )
    scores = jnp.einsum("slhe,smhe->shlm", f_query, f_key, preferred_element_type=jnp.float32)
    causal = jnp.arange(span)[:, None] >= jnp.arange(span)[None, :]
    scores = jnp.where(causal, scores, 0.0)
    weights = scores.astype(jnp.bfloat16)
    numer = jnp.einsum("shlm,smhf->slhf", weights, values, preferred_element_type=jnp.float32)
    numer = numer + jnp.einsum(
        "slhe,shef->slhf",
        f_query,
        prior_state.astype(jnp.bfloat16),
        preferred_element_type=jnp.float32,
    )
    denom = jnp.transpose(jnp.sum(scores, axis=-1), (0, 2, 1))
    denom = denom + jnp.einsum("slhe,she->slh", f_query.astype(jnp.float32), prior_norm)
    attended = (numer / denom[..., None]).astype(jnp.bfloat16).reshape(count * span, width)
    layer_out = rows.astype(jnp.float32) + jnp.dot(
        attended, w_out, preferred_element_type=jnp.float32
    )
    position = lax.axis_index("seq") * span + jnp.arange(span)
    flat_len = lengths.reshape(count)
    valid = (position[None, :] < flat_len[:, None]).astype(jnp.float32)
    pooled = jnp.sum(layer_out.reshape(count, span, width) * valid[:, :, None], axis=1)
    pooled = lax.psum(pooled, "seq")
    embed = pooled / flat_len[:, None].astype(jnp.float32)
    full_cov = lax.all_gather(running_cov, "seq", axis=0, tiled=True)
    total = lax.axis_size("dp") * count
    own_outer = jnp.dot(
        embed.T, embed, precision=lax.Precision.HIGHEST, preferred_element_type=jnp.float32
    )
    sum_embed, second = lax.psum((jnp.sum(embed, axis=0), own_outer), "dp")
    cov_full, whitened = whiten_rows(full_cov, sum_embed, second, total, embed)
    loss = lax.psum(pair_terms(whitened), "dp") / (pairs * lax.axis_size("dp"))
    share = running_cov.shape[0]
    cov_rows = lax.dynamic_slice_in_dim(cov_full, lax.axis_index("seq") * share, share, 0)
    return (whitened.reshape(pairs, two, width), cov_rows, loss)


def solution(mesh):
    placed = (P("dp", None, "seq", None), P("dp", None), P(), P(), P(), P(), P("seq", None))
    return jax.shard_map(
        body,
        mesh=mesh,
        in_specs=placed,
        out_specs=(P("dp", None, None), P("seq", None), P()),
        check_vma=False,
    )
```

profile of v0, /device:TPU:0, one launch (start us, length us, event | category | flops | bytes accessed | tf_op | source)
XLA Modules:
  0.0 632.7 jit_solution(18064278824719180027)
XLA Ops:
  9.6 2.7 select_convert_fusion.2
  14.5 3.0 select_convert_fusion.3
  17.6 2.4 reshape.210
  19.9 3.5 copy.35
  23.5 2.8 convolution_convert_fusion
  26.3 2.4 reshape.209
  28.7 2.8 copy.37
  32.5 41.2 %while.13 = (s32[]{:T(128)}, f32[2,16,64,64]{3,2,1,0:T(8,128)S(1)}, f32[2,16,64]{2,1,0:T(8,128)S(1)}, f32[2,16,64,64]{3,2,1,0:T(8,128)S(1)}, f32[2,16,64]{2,1,0:T(8,128)S(1)}, /*index=5*/s32[]{:T(128)}) while((s32[]{:T(128)}, f32[2,16,64,64]{3,2,1,0:T(8,128)S(1)}, f32[2,16,64]{2,1,0:T(8,128)S(1)}, f32[2,16,64,64]{3,2,1,0:T(8,128)S(1)}, ...), condition=%wide.region_2.3_spmd, body=%wide.region_1.2_spmd.sunk | while | flops 133122 | bytes 3727509 | solution.py:59
  32.6 2.4 collective-permute-start
  35.1 4.5 collective-permute-start.1
  40.5 11.1 %collective-permute-start = (f32[2,16,64,64]{3,2,1,0:T(8,128)S(1)}, f32[2,16,64,64]{3,2,1,0:T(8,128)S(1)}, u32[]{:S(2)}, u32[]{:S(2)}) collective-permute-start(f32[2,16,64,64]{3,2,1,0:T(8,128)S(1)} %add.171), channel_id=1, source_target_pairs={{0,1},{1,2},{2,3},{4,5},{5,6},{6,7},{8,9},{9,10},{10,11},{12,13},{... | collective-permute-start | bytes 1572872 | tf_op jit(solution)/shard_map/while/body/eval_jaxpr/ppermute | solution.py:13
  51.7 4.3 collective-permute-start.1
  57.0 11.1 %collective-permute-start = (f32[2,16,64,64]{3,2,1,0:T(8,128)S(1)}, f32[2,16,64,64]{3,2,1,0:T(8,128)S(1)}, u32[]{:S(2)}, u32[]{:S(2)}) collective-permute-start(f32[2,16,64,64]{3,2,1,0:T(8,128)S(1)} %add.171), channel_id=1, source_target_pairs={{0,1},{1,2},{2,3},{4,5},{5,6},{6,7},{8,9},{9,10},{10,11},{12,13},{... | collective-permute-start | bytes 1572872 | tf_op jit(solution)/shard_map/while/body/eval_jaxpr/ppermute | solution.py:13
  68.1 4.3 collective-permute-start.1
  82.6 15.1 %psum.28 = f32[2,1024]{1,0:T(2,128)S(1)} all-reduce(f32[2,1024]{1,0:T(2,128)S(1)} %multiply_reduce_fusion), channel_id=1, replica_groups=mesh['dp'=8,'seq'=4] {'seq'}, use_global_device_ids=true, to_apply=%region_5.6 | all-reduce | flops 2048 | bytes 16384 | tf_op jit(solution)/shard_map/psum | solution.py:83
  97.8 5.1 fusion.80
  103.5 22.2 %psum.30 = f32[1024]{0:T(1024)S(1)} all-reduce(f32[1024]{0:T(1024)S(1)} %get-tuple-element.64), channel_id=1, replica_groups=mesh['dp'=8,'seq'=4] {'dp'}, use_global_device_ids=true, to_apply=%region_8.9 | all-reduce | flops 1024 | bytes 8192 | tf_op jit(solution)/shard_map/psum | solution.py:90
  125.7 135.8 %all-reduce.3.cloned.1.call-done = f32[1024,1024]{1,0:T(8,128)} async-done(((f32[1024,1024]{1,0:T(8,128)}), f32[1024,1024]{1,0:T(8,128)}) %all-reduce.3.cloned.1.call-update) | async-done | bytes 4194320 | tf_op jit(solution)/shard_map/psum | solution.py:90
  261.5 6.2 multiply_add_fusion
  267.7 5.5 copy.45
  273.2 4.4 fusion.1
  279.6 11.7 %cholesky.223 = f32[128,128]{1,0:T(8,128)S(1)} custom-call(f32[128,128]{1,0:T(8,128)S(1)} %cholesky.580), custom_call_target="Cholesky" | custom-call | tf_op jit(solution)/shard_map/jit(cholesky)/cholesky | solution.py:24
  291.3 2.5 cholesky.255
  293.8 9.8 %custom-call.62 = f32[1,128,128]{1,2,0:T(8,128)S(1)} custom-call(f32[1,128,128]{2,1,0:T(8,128)S(1)} %get-tuple-element.89), custom_call_target="InvertDiagBlocksLowerTriangular" | custom-call | tf_op jit(solution)/shard_map/jit(cholesky)/cholesky | solution.py:24
  303.7 2.3 constant_dynamic-update-slice_fusion.31
  307.6 11.9 %cholesky.244 = f32[128,128]{1,0:T(8,128)S(1)} custom-call(f32[128,128]{1,0:T(8,128)S(1)} %cholesky.584), custom_call_target="Cholesky" | custom-call | tf_op jit(solution)/shard_map/jit(cholesky)/cholesky | solution.py:24
  320.1 9.8 %custom-call.63 = f32[1,128,128]{1,2,0:T(8,128)S(1)} custom-call(f32[1,128,128]{2,1,0:T(8,128)S(1)} %get-tuple-element.86), custom_call_target="InvertDiagBlocksLowerTriangular" | custom-call | tf_op jit(solution)/shard_map/jit(cholesky)/cholesky | solution.py:24
  333.3 11.7 %cholesky.468 = f32[128,128]{1,0:T(8,128)S(1)} custom-call(f32[128,128]{1,0:T(8,128)S(1)} %cholesky.589), custom_call_target="Cholesky" | custom-call | tf_op jit(solution)/shard_map/jit(cholesky)/cholesky | solution.py:24
  346.3 9.8 %custom-call.64 = f32[1,128,128]{1,2,0:T(8,128)S(1)} custom-call(f32[1,128,128]{2,1,0:T(8,128)S(1)} %get-tuple-element.83), custom_call_target="InvertDiagBlocksLowerTriangular" | custom-call | tf_op jit(solution)/shard_map/jit(cholesky)/cholesky | solution.py:24
  357.3 2.3 convolution_subtract_fusion.2
  359.7 12.1 %cholesky.487 = f32[128,128]{1,0:T(8,128)S(1)} custom-call(f32[128,128]{1,0:T(8,128)S(1)} %cholesky.594), custom_call_target="Cholesky" | custom-call | tf_op jit(solution)/shard_map/jit(cholesky)/cholesky | solution.py:24
  373.1 9.8 %custom-call.65 = f32[1,128,128]{1,2,0:T(8,128)S(1)} custom-call(f32[1,128,128]{2,1,0:T(8,128)S(1)} %get-tuple-element.80), custom_call_target="InvertDiagBlocksLowerTriangular" | custom-call | tf_op jit(solution)/shard_map/jit(cholesky)/cholesky | solution.py:24
  384.0 2.4 convolution_subtract_fusion.3
  386.4 11.7 %cholesky.506 = f32[128,128]{1,0:T(8,128)S(1)} custom-call(f32[128,128]{1,0:T(8,128)S(1)} %cholesky.599), custom_call_target="Cholesky" | custom-call | tf_op jit(solution)/shard_map/jit(cholesky)/cholesky | solution.py:24
  399.5 9.9 %custom-call.66 = f32[1,128,128]{1,2,0:T(8,128)S(1)} custom-call(f32[1,128,128]{2,1,0:T(8,128)S(1)} %get-tuple-element.77), custom_call_target="InvertDiagBlocksLowerTriangular" | custom-call | tf_op jit(solution)/shard_map/jit(cholesky)/cholesky | solution.py:24
  412.7 11.7 %cholesky.526 = f32[128,128]{1,0:T(8,128)S(1)} custom-call(f32[128,128]{1,0:T(8,128)S(1)} %cholesky.604), custom_call_target="Cholesky" | custom-call | tf_op jit(solution)/shard_map/jit(cholesky)/cholesky | solution.py:24
  425.8 9.8 %custom-call.67 = f32[1,128,128]{1,2,0:T(8,128)S(1)} custom-call(f32[1,128,128]{2,1,0:T(8,128)S(1)} %get-tuple-element.74), custom_call_target="InvertDiagBlocksLowerTriangular" | custom-call | tf_op jit(solution)/shard_map/jit(cholesky)/cholesky | solution.py:24
  438.6 11.9 %cholesky.546 = f32[128,128]{1,0:T(8,128)S(1)} custom-call(f32[128,128]{1,0:T(8,128)S(1)} %cholesky.609), custom_call_target="Cholesky" | custom-call | tf_op jit(solution)/shard_map/jit(cholesky)/cholesky | solution.py:24
  451.8 9.8 %custom-call.68 = f32[1,128,128]{1,2,0:T(8,128)S(1)} custom-call(f32[1,128,128]{2,1,0:T(8,128)S(1)} %get-tuple-element.71), custom_call_target="InvertDiagBlocksLowerTriangular" | custom-call | tf_op jit(solution)/shard_map/jit(cholesky)/cholesky | solution.py:24
  464.3 11.7 %cholesky.564 = f32[128,128]{1,0:T(8,128)S(1)} custom-call(f32[128,128]{1,0:T(8,128)S(1)} %convolution_subtract_fusion.6), custom_call_target="Cholesky" | custom-call | tf_op jit(solution)/shard_map/jit(cholesky)/cholesky | solution.py:24
  483.1 5.0 select_select_fusion
  488.0 23.2 %while.14 = (s32[]{:T(128)}, f32[1024,1024]{1,0:T(8,128)}, s32[8,2]{0,1:T(2,128)S(1)}, f32[8,128,128]{2,1,0:T(8,128)S(1)}, s32[]{:T(128)}) while((s32[]{:T(128)}, f32[1024,1024]{1,0:T(8,128)}, s32[8,2]{0,1:T(2,128)S(1)}, f32[8,128,128]{2,1,0:T(8,128)S(1)}, s32[]{:T(128)}) %tuple.81), condition=%wide.while_cond, body=%wide.while_body.sunk | while | flops 2 | bytes 131189 | solution.py:25
  488.6 2.3 bitcast_dynamic-update-slice_fusion.2
  494.5 2.3 bitcast_dynamic-update-slice_fusion.2
  497.4 2.3 bitcast_dynamic-update-slice_fusion.2
  511.2 78.6 %custom-call.69 = f32[8,128,128]{1,2,0:T(8,128)S(1)} custom-call(f32[8,128,128]{2,1,0:T(8,128)S(1)} %get-tuple-element.40), custom_call_target="InvertDiagBlocksLowerTriangular" | custom-call | tf_op jit(solution)/shard_map/triangular_solve | solution.py:25
  601.2 2.3 constant_dynamic-slice_fusion.1
  603.5 19.7 %psum.31 = f32[]{:T(128)} all-reduce(f32[]{:T(128)} %fusion.63), channel_id=1, replica_groups=mesh['dp'=8,'seq'=4] {'dp'}, use_global_device_ids=true, to_apply=%region_27.28 | all-reduce | flops 1 | bytes 8 | tf_op jit(solution)/shard_map/psum | solution.py:92
  (141 shorter events, 72.0 us)
Async XLA Ops:
  8.0 1.6 copy-start
  8.0 253.5 %all-reduce.3.cloned.1.call-start = ((), (), s32[]{:S(2)}) async-start(), calls=%async_computation.1 | async-start | bytes 8388608 | tf_op jit(solution)/shard_map/psum | solution.py:90
  12.8 1.7 copy-start.9
  13.1 18.4 %copy-start.3 = (bf16[2,256,16,64]{1,0,3,2:T(2,128)(2,1)}, bf16[2,256,16,64]{1,0,3,2:T(2,128)(2,1)S(1)}, u32[]{:S(2)}) copy-start(bf16[2,256,16,64]{1,0,3,2:T(2,128)(2,1)S(1)} %reshape.179) | copy-start | bytes 3145732
  31.5 1.0 copy-start.6
  32.6 7.7 %collective-permute-start = (f32[2,16,64,64]{3,2,1,0:T(8,128)S(1)}, f32[2,16,64,64]{3,2,1,0:T(8,128)S(1)}, u32[]{:S(2)}, u32[]{:S(2)}) collective-permute-start(f32[2,16,64,64]{3,2,1,0:T(8,128)S(1)} %add.171), channel_id=1, source_target_pairs={{0,1},{1,2},{2,3},{4,5},{5,6},{6,7},{8,9},{9,10},{10,11},{12,13},{... | collective-permute-start | bytes 1572872 | tf_op jit(solution)/shard_map/while/body/eval_jaxpr/ppermute | solution.py:13
  35.1 5.3 collective-permute-start.1
  40.5 16.3 %collective-permute-start = (f32[2,16,64,64]{3,2,1,0:T(8,128)S(1)}, f32[2,16,64,64]{3,2,1,0:T(8,128)S(1)}, u32[]{:S(2)}, u32[]{:S(2)}) collective-permute-start(f32[2,16,64,64]{3,2,1,0:T(8,128)S(1)} %add.171), channel_id=1, source_target_pairs={{0,1},{1,2},{2,3},{4,5},{5,6},{6,7},{8,9},{9,10},{10,11},{12,13},{... | collective-permute-start | bytes 1572872 | tf_op jit(solution)/shard_map/while/body/eval_jaxpr/ppermute | solution.py:13
  51.7 5.2 collective-permute-start.1
  57.0 16.3 %collective-permute-start = (f32[2,16,64,64]{3,2,1,0:T(8,128)S(1)}, f32[2,16,64,64]{3,2,1,0:T(8,128)S(1)}, u32[]{:S(2)}, u32[]{:S(2)}) collective-permute-start(f32[2,16,64,64]{3,2,1,0:T(8,128)S(1)} %add.171), channel_id=1, source_target_pairs={{0,1},{1,2},{2,3},{4,5},{5,6},{6,7},{8,9},{9,10},{10,11},{12,13},{... | collective-permute-start | bytes 1572872 | tf_op jit(solution)/shard_map/while/body/eval_jaxpr/ppermute | solution.py:13
  68.1 5.2 collective-permute-start.1
  73.7 3.4 copy-start.4
  73.7 3.4 copy-start.5
  77.1 1.4 copy-start.7
  79.4 1.4 copy-start.12
  79.4 1.6 copy-start.8
  79.4 1.9 copy-start.10
  102.9 158.6 %all-gather.2.cloned.1.call-start = ((), (), s32[]{:S(2)}) async-start(), calls=%async_computation | async-start | bytes 5242880 | tf_op jit(solution)/shard_map/all_gather | solution.py:85
  277.6 2.0 copy-start.2
  483.0 140.8 %copy-start.1 = (bf16[1024,1024]{1,0:T(8,128)(2,1)S(1)}, bf16[1024,1024]{1,0:T(8,128)(2,1)}, u32[]{:S(2)}) copy-start(bf16[1024,1024]{1,0:T(8,128)(2,1)} %param.12) | copy-start | bytes 6291460
  600.3 23.5 %copy-start.11 = (f32[1024,2]{0,1:T(2,128)}, f32[1024,2]{0,1:T(2,128)S(1)}, u32[]{:S(2)}) copy-start(f32[1024,2]{0,1:T(2,128)S(1)} %convolution_dynamic-update-slice_fusion.6) | copy-start | bytes 24580
Sparse Core Ops, SparseCore 0:
  103.0 158.4 all-reduce.2
Sparse Core Ops, SparseCore 1:
  104.9 36.3 all-gather.1
where the time goes:
time: 641 us; the launch traced here: 633 us
  other arithmetic  270 us (42%)
  waiting for transfers between devices  139 us (22%)
  blocking collectives  57 us (9%)
  matrix products  54.5 us (9%)
  local copies, waits for them, and re-layouts  50.5 us (8%)
  starting transfers between devices  37.9 us (6%)
  between operations  23.1 us (4%)
    another operation x30, other arithmetic, whiten_rows(): chol = jnp.linalg.cholesky(cov_full)  173 us
    psum x1, waiting for transfers between devices, body(): sum_embed, second = lax.psum((jnp.sum(embed, axis=0), own_outer), 'dp')  136 us
    another operation x3, other arithmetic, whiten_rows(): lax.linalg.triangular_solve(chol, (rows_in - mean).T, left_side=True, low...  83.6 us
    ppermute x6, starting transfers between devices, passed_along(): return lax.ppermute(array, axis, pairs)  37.8 us
    another operation x14, matrix products, whiten_rows(): chol = jnp.linalg.cholesky(cov_full)  23.1 us
    another operation x24, local copies, waits for them, and re-layouts  23 us
    psum x1, blocking collectives, body(): sum_embed, second = lax.psum((jnp.sum(embed, axis=0), own_outer), 'dp')  22.2 us
    psum x1, blocking collectives, body(): loss = lax.psum(pair_terms(whitened), 'dp') / (pairs * lax.axis_size('dp'))  19.7 us
  transfers between devices with their start and end apart: 8, of which 4 were waited for; matrix products, arithmetic and copies ran while one was open for 0% of the time, Pallas kernels for 0%

commit v1 on v0

--- a/solution.py
+++ b/solution.py
@@ -2,9 +2,21 @@
 import jax.numpy as jnp
 from jax import lax
 from jax.sharding import PartitionSpec as P
+from jax.lax import axis_size, ppermute
 
 HEADS = 16
 HEAD_DIM = 64
+
+
+def form_ports_up(mine_x):
+    num = axis_size("seq")
+    all_rows = lambda passed: [(no, no ^ passed) for no in range(num)]
+    outcome_arr = mine_x
+    for it in range(num.bit_length() - 1):
+        ready = all_rows(1 << it)
+        m_next = ppermute(outcome_arr, axis_name="seq", perm=ready)
+        outcome_arr = outcome_arr + m_next
+    return outcome_arr
 
 
 def passed_along(array, axis, by):
@@ -80,7 +92,7 @@
     flat_len = lengths.reshape(count)
     valid = (position[None, :] < flat_len[:, None]).astype(jnp.float32)
     pooled = jnp.sum(layer_out.reshape(count, span, width) * valid[:, :, None], axis=1)
-    pooled = lax.psum(pooled, "seq")
+    pooled = form_ports_up(pooled)
     embed = pooled / flat_len[:, None].astype(jnp.float32)
     full_cov = lax.all_gather(running_cov, "seq", axis=0, tiled=True)
     total = lax.axis_size("dp") * count

time: 641 us -> 640 us (level)
  blocking collectives: 57 us -> 42.1 us
  starting transfers between devices: 37.9 us -> 49.8 us
    psum x1 -> x0, blocking collectives: 15.1 us -> none  [body(): pooled = lax.psum(pooled, 'seq')]
    ppermute x0 -> x2, starting transfers between devices: none -> 11.9 us  [form_ports_up(): m_next = ppermute(outcome_arr, axis_name='seq', perm=ready)]
  transfers between devices with their start and end apart: 8 -> 10, of which waited for: 4 -> 6; matrix products, arithmetic and copies ran while one was open for 0% -> 0% of each run, Pallas kernels for 0% -> 0%
where the time goes in v1:
time: 640 us; the launch traced here: 632 us
  other arithmetic  269 us (42%)
  waiting for transfers between devices  141 us (22%)
  matrix products  54.5 us (9%)
  local copies, waits for them, and re-layouts  51.3 us (8%)
  starting transfers between devices  49.8 us (8%)
  blocking collectives  42.1 us (7%)
  between operations  23.1 us (4%)
    another operation x30, other arithmetic, whiten_rows(): chol = jnp.linalg.cholesky(cov_full)  173 us
    psum x1, waiting for transfers between devices, body(): sum_embed, second = lax.psum((jnp.sum(embed, axis=0), own_outer), 'dp')  135 us
    another operation x3, other arithmetic, whiten_rows(): lax.linalg.triangular_solve(chol, (rows_in - mean).T, left_side=True, low...  83.6 us
    ppermute x6, starting transfers between devices, passed_along(): return lax.ppermute(array, axis, pairs)  37.8 us
    another operation x14, matrix products, whiten_rows(): chol = jnp.linalg.cholesky(cov_full)  23.1 us
    another operation x24, local copies, waits for them, and re-layouts  23 us
    psum x1, blocking collectives, body(): sum_embed, second = lax.psum((jnp.sum(embed, axis=0), own_outer), 'dp')  22.4 us
    psum x1, blocking collectives, body(): loss = lax.psum(pair_terms(whitened), 'dp') / (pairs * lax.axis_size('dp'))  19.7 us
  transfers between devices with their start and end apart: 10, of which 6 were waited for; matrix products, arithmetic and copies ran while one was open for 0% of the time, Pallas kernels for 0%

profile of v1, /device:TPU:0, one launch (start us, length us, event | category | flops | bytes accessed | tf_op | source)
XLA Modules:
  0.0 631.6 jit_solution(9357885682753353353)
XLA Ops:
  9.6 2.7 select_convert_fusion.2
  14.5 3.0 select_convert_fusion.3
  17.6 2.4 reshape.210
  19.9 3.5 copy.35
  23.5 2.8 convolution_convert_fusion
  26.3 2.4 reshape.209
  28.7 2.8 copy.37
  32.5 41.2 %while.13 = (s32[]{:T(128)}, f32[2,16,64,64]{3,2,1,0:T(8,128)S(1)}, f32[2,16,64]{2,1,0:T(8,128)S(1)}, f32[2,16,64,64]{3,2,1,0:T(8,128)S(1)}, f32[2,16,64]{2,1,0:T(8,128)S(1)}, /*index=5*/s32[]{:T(128)}) while((s32[]{:T(128)}, f32[2,16,64,64]{3,2,1,0:T(8,128)S(1)}, f32[2,16,64]{2,1,0:T(8,128)S(1)}, f32[2,16,64,64]{3,2,1,0:T(8,128)S(1)}, ...), condition=%wide.region_2.3_spmd, body=%wide.region_1.2_spmd.sunk | while | flops 133122 | bytes 3727509 | solution.py:71
  32.6 2.4 collective-permute-start
  35.1 4.5 collective-permute-start.1
  40.5 11.1 %collective-permute-start = (f32[2,16,64,64]{3,2,1,0:T(8,128)S(1)}, f32[2,16,64,64]{3,2,1,0:T(8,128)S(1)}, u32[]{:S(2)}, u32[]{:S(2)}) collective-permute-start(f32[2,16,64,64]{3,2,1,0:T(8,128)S(1)} %add.179), channel_id=1, source_target_pairs={{0,1},{1,2},{2,3},{4,5},{5,6},{6,7},{8,9},{9,10},{10,11},{12,13},{... | collective-permute-start | bytes 1572872 | tf_op jit(solution)/shard_map/while/body/eval_jaxpr/ppermute | solution.py:25
  51.7 4.3 collective-permute-start.1
  57.0 11.1 %collective-permute-start = (f32[2,16,64,64]{3,2,1,0:T(8,128)S(1)}, f32[2,16,64,64]{3,2,1,0:T(8,128)S(1)}, u32[]{:S(2)}, u32[]{:S(2)}) collective-permute-start(f32[2,16,64,64]{3,2,1,0:T(8,128)S(1)} %add.179), channel_id=1, source_target_pairs={{0,1},{1,2},{2,3},{4,5},{5,6},{6,7},{8,9},{9,10},{10,11},{12,13},{... | collective-permute-start | bytes 1572872 | tf_op jit(solution)/shard_map/while/body/eval_jaxpr/ppermute | solution.py:25
  68.1 4.3 collective-permute-start.1
  82.6 9.2 %collective-permute-start.2 = (f32[2,1024]{1,0:T(2,128)S(1)}, f32[2,1024]{1,0:T(2,128)S(1)}, u32[]{:S(2)}, u32[]{:S(2)}) collective-permute-start(f32[2,1024]{1,0:T(2,128)S(1)} %multiply_reduce_fusion), channel_id=1, source_target_pairs={{0,1},{1,0},{2,3},{3,2},{4,5},{5,4},{6,7},{7,6},{8,9},{9,8},{10,11... | collective-permute-start | bytes 24584 | tf_op jit(solution)/shard_map/ppermute | solution.py:17
  92.6 2.7 collective-permute-start.3
  97.0 5.1 fusion.87
  102.7 22.4 %psum.22 = f32[1024]{0:T(1024)S(1)} all-reduce(f32[1024]{0:T(1024)S(1)} %get-tuple-element.64), channel_id=1, replica_groups=mesh['dp'=8,'seq'=4] {'dp'}, use_global_device_ids=true, to_apply=%region_7.8 | all-reduce | flops 1024 | bytes 8192 | tf_op jit(solution)/shard_map/psum | solution.py:102
  125.2 135.3 %all-reduce.3.cloned.1.call-done = f32[1024,1024]{1,0:T(8,128)} async-done(((f32[1024,1024]{1,0:T(8,128)}), f32[1024,1024]{1,0:T(8,128)}) %all-reduce.3.cloned.1.call-update) | async-done | bytes 4194320 | tf_op jit(solution)/shard_map/psum | solution.py:102
  260.5 6.2 multiply_add_fusion
  266.6 5.5 copy.45
  272.1 4.4 fusion.1
  278.5 11.7 %cholesky.223 = f32[128,128]{1,0:T(8,128)S(1)} custom-call(f32[128,128]{1,0:T(8,128)S(1)} %cholesky.580), custom_call_target="Cholesky" | custom-call | tf_op jit(solution)/shard_map/jit(cholesky)/cholesky | solution.py:36
  290.3 2.5 cholesky.255
  292.8 9.8 %custom-call.62 = f32[1,128,128]{1,2,0:T(8,128)S(1)} custom-call(f32[1,128,128]{2,1,0:T(8,128)S(1)} %get-tuple-element.89), custom_call_target="InvertDiagBlocksLowerTriangular" | custom-call | tf_op jit(solution)/shard_map/jit(cholesky)/cholesky | solution.py:36
  302.6 2.3 constant_dynamic-update-slice_fusion.31
  306.5 11.9 %cholesky.244 = f32[128,128]{1,0:T(8,128)S(1)} custom-call(f32[128,128]{1,0:T(8,128)S(1)} %cholesky.584), custom_call_target="Cholesky" | custom-call | tf_op jit(solution)/shard_map/jit(cholesky)/cholesky | solution.py:36
  319.1 9.8 %custom-call.63 = f32[1,128,128]{1,2,0:T(8,128)S(1)} custom-call(f32[1,128,128]{2,1,0:T(8,128)S(1)} %get-tuple-element.86), custom_call_target="InvertDiagBlocksLowerTriangular" | custom-call | tf_op jit(solution)/shard_map/jit(cholesky)/cholesky | solution.py:36
  332.2 11.7 %cholesky.468 = f32[128,128]{1,0:T(8,128)S(1)} custom-call(f32[128,128]{1,0:T(8,128)S(1)} %cholesky.589), custom_call_target="Cholesky" | custom-call | tf_op jit(solution)/shard_map/jit(cholesky)/cholesky | solution.py:36
  345.3 9.8 %custom-call.64 = f32[1,128,128]{1,2,0:T(8,128)S(1)} custom-call(f32[1,128,128]{2,1,0:T(8,128)S(1)} %get-tuple-element.83), custom_call_target="InvertDiagBlocksLowerTriangular" | custom-call | tf_op jit(solution)/shard_map/jit(cholesky)/cholesky | solution.py:36
  356.2 2.3 convolution_subtract_fusion.2
  358.6 12.1 %cholesky.487 = f32[128,128]{1,0:T(8,128)S(1)} custom-call(f32[128,128]{1,0:T(8,128)S(1)} %cholesky.594), custom_call_target="Cholesky" | custom-call | tf_op jit(solution)/shard_map/jit(cholesky)/cholesky | solution.py:36
  372.0 9.8 %custom-call.65 = f32[1,128,128]{1,2,0:T(8,128)S(1)} custom-call(f32[1,128,128]{2,1,0:T(8,128)S(1)} %get-tuple-element.80), custom_call_target="InvertDiagBlocksLowerTriangular" | custom-call | tf_op jit(solution)/shard_map/jit(cholesky)/cholesky | solution.py:36
  382.9 2.4 convolution_subtract_fusion.3
  385.3 11.7 %cholesky.506 = f32[128,128]{1,0:T(8,128)S(1)} custom-call(f32[128,128]{1,0:T(8,128)S(1)} %cholesky.599), custom_call_target="Cholesky" | custom-call | tf_op jit(solution)/shard_map/jit(cholesky)/cholesky | solution.py:36
  398.4 9.9 %custom-call.66 = f32[1,128,128]{1,2,0:T(8,128)S(1)} custom-call(f32[1,128,128]{2,1,0:T(8,128)S(1)} %get-tuple-element.77), custom_call_target="InvertDiagBlocksLowerTriangular" | custom-call | tf_op jit(solution)/shard_map/jit(cholesky)/cholesky | solution.py:36
  411.7 11.7 %cholesky.526 = f32[128,128]{1,0:T(8,128)S(1)} custom-call(f32[128,128]{1,0:T(8,128)S(1)} %cholesky.604), custom_call_target="Cholesky" | custom-call | tf_op jit(solution)/shard_map/jit(cholesky)/cholesky | solution.py:36
  424.7 9.8 %custom-call.67 = f32[1,128,128]{1,2,0:T(8,128)S(1)} custom-call(f32[1,128,128]{2,1,0:T(8,128)S(1)} %get-tuple-element.74), custom_call_target="InvertDiagBlocksLowerTriangular" | custom-call | tf_op jit(solution)/shard_map/jit(cholesky)/cholesky | solution.py:36
  437.5 11.9 %cholesky.546 = f32[128,128]{1,0:T(8,128)S(1)} custom-call(f32[128,128]{1,0:T(8,128)S(1)} %cholesky.609), custom_call_target="Cholesky" | custom-call | tf_op jit(solution)/shard_map/jit(cholesky)/cholesky | solution.py:36
  450.7 9.8 %custom-call.68 = f32[1,128,128]{1,2,0:T(8,128)S(1)} custom-call(f32[1,128,128]{2,1,0:T(8,128)S(1)} %get-tuple-element.71), custom_call_target="InvertDiagBlocksLowerTriangular" | custom-call | tf_op jit(solution)/shard_map/jit(cholesky)/cholesky | solution.py:36
  463.2 11.7 %cholesky.564 = f32[128,128]{1,0:T(8,128)S(1)} custom-call(f32[128,128]{1,0:T(8,128)S(1)} %convolution_subtract_fusion.6), custom_call_target="Cholesky" | custom-call | tf_op jit(solution)/shard_map/jit(cholesky)/cholesky | solution.py:36
  482.0 5.0 select_select_fusion
  487.0 23.2 %while.14 = (s32[]{:T(128)}, f32[1024,1024]{1,0:T(8,128)}, s32[8,2]{0,1:T(2,128)S(1)}, f32[8,128,128]{2,1,0:T(8,128)S(1)}, s32[]{:T(128)}) while((s32[]{:T(128)}, f32[1024,1024]{1,0:T(8,128)}, s32[8,2]{0,1:T(2,128)S(1)}, f32[8,128,128]{2,1,0:T(8,128)S(1)}, s32[]{:T(128)}) %tuple.81), condition=%wide.while_cond, body=%wide.while_body.sunk | while | flops 2 | bytes 131189 | solution.py:37
  490.5 2.3 bitcast_dynamic-update-slice_fusion.2
  493.4 2.3 bitcast_dynamic-update-slice_fusion.2
  510.2 78.6 %custom-call.69 = f32[8,128,128]{1,2,0:T(8,128)S(1)} custom-call(f32[8,128,128]{2,1,0:T(8,128)S(1)} %get-tuple-element.40), custom_call_target="InvertDiagBlocksLowerTriangular" | custom-call | tf_op jit(solution)/shard_map/triangular_solve | solution.py:37
  600.1 2.3 constant_dynamic-slice_fusion.1
  602.4 19.7 %psum.23 = f32[]{:T(128)} all-reduce(f32[]{:T(128)} %fusion.70), channel_id=1, replica_groups=mesh['dp'=8,'seq'=4] {'dp'}, use_global_device_ids=true, to_apply=%region_26.27 | all-reduce | flops 1 | bytes 8 | tf_op jit(solution)/shard_map/psum | solution.py:104
  (145 shorter events, 76.7 us)
Async XLA Ops:
  8.0 1.6 copy-start
  8.0 252.4 %all-reduce.3.cloned.1.call-start = ((), (), s32[]{:S(2)}) async-start(), calls=%async_computation.1 | async-start | bytes 8388608 | tf_op jit(solution)/shard_map/psum | solution.py:102
  12.8 1.7 copy-start.9
  13.1 18.4 %copy-start.3 = (bf16[2,256,16,64]{1,0,3,2:T(2,128)(2,1)}, bf16[2,256,16,64]{1,0,3,2:T(2,128)(2,1)S(1)}, u32[]{:S(2)}) copy-start(bf16[2,256,16,64]{1,0,3,2:T(2,128)(2,1)S(1)} %reshape.179) | copy-start | bytes 3145732
  31.5 1.0 copy-start.6
  32.6 7.7 %collective-permute-start = (f32[2,16,64,64]{3,2,1,0:T(8,128)S(1)}, f32[2,16,64,64]{3,2,1,0:T(8,128)S(1)}, u32[]{:S(2)}, u32[]{:S(2)}) collective-permute-start(f32[2,16,64,64]{3,2,1,0:T(8,128)S(1)} %add.179), channel_id=1, source_target_pairs={{0,1},{1,2},{2,3},{4,5},{5,6},{6,7},{8,9},{9,10},{10,11},{12,13},{... | collective-permute-start | bytes 1572872 | tf_op jit(solution)/shard_map/while/body/eval_jaxpr/ppermute | solution.py:25
  35.1 5.3 collective-permute-start.1
  40.5 16.3 %collective-permute-start = (f32[2,16,64,64]{3,2,1,0:T(8,128)S(1)}, f32[2,16,64,64]{3,2,1,0:T(8,128)S(1)}, u32[]{:S(2)}, u32[]{:S(2)}) collective-permute-start(f32[2,16,64,64]{3,2,1,0:T(8,128)S(1)} %add.179), channel_id=1, source_target_pairs={{0,1},{1,2},{2,3},{4,5},{5,6},{6,7},{8,9},{9,10},{10,11},{12,13},{... | collective-permute-start | bytes 1572872 | tf_op jit(solution)/shard_map/while/body/eval_jaxpr/ppermute | solution.py:25
  51.7 5.2 collective-permute-start.1
  57.0 16.3 %collective-permute-start = (f32[2,16,64,64]{3,2,1,0:T(8,128)S(1)}, f32[2,16,64,64]{3,2,1,0:T(8,128)S(1)}, u32[]{:S(2)}, u32[]{:S(2)}) collective-permute-start(f32[2,16,64,64]{3,2,1,0:T(8,128)S(1)} %add.179), channel_id=1, source_target_pairs={{0,1},{1,2},{2,3},{4,5},{5,6},{6,7},{8,9},{9,10},{10,11},{12,13},{... | collective-permute-start | bytes 1572872 | tf_op jit(solution)/shard_map/while/body/eval_jaxpr/ppermute | solution.py:25
  68.1 5.2 collective-permute-start.1
  73.7 3.4 copy-start.4
  73.7 3.4 copy-start.5
  77.1 1.4 copy-start.7
  79.4 1.4 copy-start.12
  79.4 1.6 copy-start.8
  79.4 1.9 copy-start.10
  82.6 10.0 %collective-permute-start.2 = (f32[2,1024]{1,0:T(2,128)S(1)}, f32[2,1024]{1,0:T(2,128)S(1)}, u32[]{:S(2)}, u32[]{:S(2)}) collective-permute-start(f32[2,1024]{1,0:T(2,128)S(1)} %multiply_reduce_fusion), channel_id=1, source_target_pairs={{0,1},{1,0},{2,3},{3,2},{4,5},{5,4},{6,7},{7,6},{8,9},{9,8},{10,11... | collective-permute-start | bytes 24584 | tf_op jit(solution)/shard_map/ppermute | solution.py:17
  92.6 4.3 collective-permute-start.3
  102.1 158.3 %all-gather.2.cloned.1.call-start = ((), (), s32[]{:S(2)}) async-start(), calls=%async_computation | async-start | bytes 5242880 | tf_op jit(solution)/shard_map/all_gather | solution.py:97
  276.5 2.0 copy-start.2
  482.0 140.8 %copy-start.1 = (bf16[1024,1024]{1,0:T(8,128)(2,1)S(1)}, bf16[1024,1024]{1,0:T(8,128)(2,1)}, u32[]{:S(2)}) copy-start(bf16[1024,1024]{1,0:T(8,128)(2,1)} %param.12) | copy-start | bytes 6291460
  599.3 23.5 %copy-start.11 = (f32[1024,2]{0,1:T(2,128)}, f32[1024,2]{0,1:T(2,128)S(1)}, u32[]{:S(2)}) copy-start(f32[1024,2]{0,1:T(2,128)S(1)} %convolution_dynamic-update-slice_fusion.6) | copy-start | bytes 24580
Sparse Core Ops, SparseCore 0:
  102.3 158.1 all-reduce.2
Sparse Core Ops, SparseCore 1:
  104.2 36.0 all-gather.1
